TPU v7x, 128 devices: a whole 4x4x4 slice. The times are simulated.
128 devices in a mesh: leaf: 8 (over y, core), front: 16 (over z, x).
Axes of the slice: x: 4, y: 4, z: 4, core: 2. Of those that a mesh axis runs over, the one named last changes fastest.
Arguments:
- front_entries: float32 [16, 8, 128, 8, 16, 128], P(None, 'leaf', None, None, 'front'), as said below
- child_panels: bfloat16 [8, 2048, 512], P('leaf', 'front'), may hold values from -0.053955078 to 0.053955078
- child_blocks: bfloat16 [8, 2048, 2048], P('leaf', None, 'front'), as said below
- child_map: int32 [8, 16], replicated, may hold values from 0 to 127, as said below
Outputs:
- factored: float32 [16, 8, 128, 8, 16, 128], P(None, 'leaf', None, None, 'front')
Inputs may be any that keep to these rules, and one draw needn't show every extreme that they name: The blocks of one subtree go to distinct parent blocks, and child_map[c, j] modulo 16 equals j. front_entries is symmetric and positive definite, with its diagonal in 6 to 9. `child_blocks`: each subtree's block is symmetric with diagonal in 6 to 9 and small independent entries elsewhere.
All inputs are finite; a program needn't handle non-finite values.
Results may differ from a plain program's by a relative error of at most 0.0012.
Values may be sent and summed in bfloat16 or wider, within the bound.
No kernel may reach another device: no remote copies, remote signals or barrier semaphores. Data moves between devices by JAX's collectives and lax.ppermute only.
A program may use at most 128 MiB of HBM per device.

v0:
```python
import jax
import jax.numpy as jnp
from jax import lax
from jax.sharding import PartitionSpec as P

KS = 8


def broadcast(x, axis, root):
    mine = lax.axis_index(axis) == root
    return lax.psum(jnp.where(mine, x, jnp.zeros_like(x)), axis)


def for_sending(x):
    return jax.tree.map(lambda a: a.astype(jnp.bfloat16) if a.dtype == jnp.float32 else a, x)


def on_device(front_entries, child_panels, child_blocks, child_map):
    leaf_count = lax.axis_size("leaf")
    front_count = lax.axis_size("front")
    leaf_id = lax.axis_index("leaf")
    front_id = lax.axis_index("front")
    row_blocks = front_entries.shape[0]
    block_size = front_entries.shape[2]
    col_blocks = front_entries.shape[3]
    spread = front_count // leaf_count
    own_rows = child_panels[0]
    own_block = child_blocks[0]
    given = own_block.astype(jnp.float32)
    product = lax.dot_general(
        lax.all_gather(child_panels[0], "front", axis=0, tiled=True),
        own_rows,
        (((1,), (1,)), ((), ())),
        preferred_element_type=jnp.float32,
    )
    update = (given - product).astype(jnp.bfloat16)
    row_targets = lax.dynamic_index_in_dim(
        child_map.reshape(leaf_count, spread, leaf_count), leaf_id, 2, keepdims=False
    )
    col_targets = lax.dynamic_index_in_dim(child_map, front_id, 1, keepdims=False)
    row_onehot = (
        row_targets[:, :, None] // leaf_count == jnp.arange(row_blocks)[None, None, :]
    ).astype(jnp.float32)
    col_onehot = (col_targets[:, None] // front_count == jnp.arange(col_blocks)[None, :]).astype(
        jnp.float32
    )
    every = lax.all_gather(update[None], "leaf", axis=0, tiled=True)
    received = lax.dynamic_index_in_dim(
        every.reshape(leaf_count, spread, leaf_count, block_size, block_size),
        leaf_id,
        2,
        keepdims=False,
    )
    added = jnp.einsum(
        "cqr,cqxy,cs->rxsy",
        row_onehot,
        received.astype(jnp.float32),
        col_onehot,
        precision=lax.Precision.HIGHEST,
    )
    assembled = front_entries.reshape(
        row_blocks * block_size, col_blocks * block_size
    ) + added.reshape(row_blocks * block_size, col_blocks * block_size)
    global_rows = jnp.arange(row_blocks) * leaf_count + leaf_id
    global_cols = jnp.arange(col_blocks) * front_count + front_id
    for pivot_index in range(KS):
        col_local = pivot_index // front_count
        col_owner = pivot_index % front_count
        row_local = pivot_index // leaf_count
        row_owner = pivot_index % leaf_count
        column = assembled[:, col_local * block_size : (col_local + 1) * block_size]
        panel = broadcast(column.astype(jnp.bfloat16), "front", col_owner).astype(column.dtype)
        pivot = broadcast(
            panel[row_local * block_size : (row_local + 1) * block_size].astype(jnp.bfloat16),
            "leaf",
            row_owner,
        ).astype(jnp.float32)
        factor = jnp.linalg.cholesky(pivot)
        solved = lax.linalg.triangular_solve(
            factor, panel, left_side=False, lower=True, transpose_a=True
        )
        keeping = (global_rows >= pivot_index).astype(jnp.float32)
        solved = (
            solved.reshape(row_blocks, block_size, block_size) * keeping[:, None, None]
        ).reshape(row_blocks * block_size, block_size)
        chosen = lax.dynamic_index_in_dim(
            solved.reshape(col_blocks, spread, block_size, block_size),
            front_id // leaf_count,
            1,
            keepdims=False,
        )
        matching = broadcast(for_sending(chosen), "leaf", front_id % leaf_count).astype(
            chosen.dtype
        )
        assembled = assembled - lax.dot_general(
            solved,
            matching.reshape(col_blocks * block_size, block_size),
            (((1,), (1,)), ((), ())),
            precision=lax.Precision.HIGHEST,
            preferred_element_type=jnp.float32,
        )
        current = assembled[:, col_local * block_size : (col_local + 1) * block_size]
        assembled = assembled.at[:, col_local * block_size : (col_local + 1) * block_size].set(
            jnp.where(front_id == col_owner, solved, current)
        )
    shaped = assembled.reshape(row_blocks, block_size, col_blocks, block_size)
    keep_rows = global_rows[:, None] >= KS
    keep_cols = global_cols[None, :] < KS
    keeping = jnp.logical_or(keep_rows, keep_cols)
    result = jnp.where(keeping[:, None, :, None], shaped, 0.0)
    return result.reshape(row_blocks, 1, block_size, col_blocks, 1, block_size)


def solution(mesh):
    placed = (
        P(None, "leaf", None, None, "front", None),
        P("leaf", "front", None),
        P("leaf", None, "front"),
        P(),
    )
    return jax.shard_map(
        on_device,
        mesh=mesh,
        in_specs=placed,
        out_specs=P(None, "leaf", None, None, "front", None),
        check_vma=False,
    )
```

profile of v0, /device:TPU:0, one launch (start us, length us, event | category | flops | bytes accessed | tf_op | source)
XLA Modules:
  0.0 1841.0 jit_solution(18026250259954352641)
XLA Ops:
  7.3 49.7 %all-gather.5.cloned.1.call-done = bf16[1,2048,512]{2,1,0:T(8,128)(2,1)} async-done(((bf16[1,128,512]{2,1,0:T(8,128)(2,1)}), bf16[1,2048,512]{2,1,0:T(8,128)(2,1)}) %all-gather.5.cloned.1.call-update) | async-done | bytes 2097168 | tf_op jit(solution)/shard_map/all_gather | solution.py:31
  103.6 25.1 %copy.29 = f32[16,128,8,128]{1,0,3,2:T(8,128)} copy(f32[16,128,8,128]{3,2,0,1:T(8,128)} %fusion.2) | data formatting | bytes 16777216 | tf_op jit(solution)/shard_map/cqr,cqxy,cs->rxsy/transpose | solution.py:54
  144.9 85.7 %all-reduce.17.cloned.1.call-done = bf16[2048,128]{0,1:T(8,128)(2,1)} async-done(((bf16[2048,128]{0,1:T(8,128)(2,1)}), bf16[2048,128]{0,1:T(8,128)(2,1)}) %all-reduce.17.cloned.1.call-update) | async-done | bytes 524304 | tf_op jit(solution)/shard_map/psum | solution.py:11
  283.7 56.6 %all-reduce.19.cloned.1.call-done = bf16[1024,128]{1,0:T(8,128)(2,1)} async-done(((bf16[1024,128]{1,0:T(8,128)(2,1)}), bf16[1024,128]{1,0:T(8,128)(2,1)}) %all-reduce.19.cloned.1.call-update) | async-done | bytes 262160 | tf_op jit(solution)/shard_map/psum | solution.py:11
  351.9 84.8 %all-reduce.21.cloned.1.call-done = bf16[2048,128]{0,1:T(8,128)(2,1)} async-done(((bf16[2048,128]{0,1:T(8,128)(2,1)}), bf16[2048,128]{0,1:T(8,128)(2,1)}) %all-reduce.21.cloned.1.call-update) | async-done | bytes 524304 | tf_op jit(solution)/shard_map/psum | solution.py:11
  437.5 24.1 %psum.172 = bf16[128,128]{0,1:T(8,128)(2,1)S(1)} all-reduce(bf16[128,128]{0,1:T(8,128)(2,1)S(1)} %slice_select_fusion.6), channel_id=1, replica_groups=mesh['leaf'=8,'front'=16] {'leaf'}, use_global_device_ids=true, to_apply=%region_7.10 | all-reduce | flops 16384 | bytes 65536 | tf_op jit(solution)/shard_map/psum | solution.py:11
  494.2 54.3 %all-reduce.23.cloned.1.call-done = bf16[1024,128]{1,0:T(8,128)(2,1)} async-done(((bf16[1024,128]{1,0:T(8,128)(2,1)}), bf16[1024,128]{1,0:T(8,128)(2,1)}) %all-reduce.23.cloned.1.call-update) | async-done | bytes 262160 | tf_op jit(solution)/shard_map/psum | solution.py:11
  560.1 84.9 %all-reduce.25.cloned.1.call-done = bf16[2048,128]{0,1:T(8,128)(2,1)} async-done(((bf16[2048,128]{0,1:T(8,128)(2,1)}), bf16[2048,128]{0,1:T(8,128)(2,1)}) %all-reduce.25.cloned.1.call-update) | async-done | bytes 524304 | tf_op jit(solution)/shard_map/psum | solution.py:11
  645.8 23.9 %psum.175 = bf16[128,128]{0,1:T(8,128)(2,1)S(1)} all-reduce(bf16[128,128]{0,1:T(8,128)(2,1)S(1)} %slice_select_fusion.5), channel_id=1, replica_groups=mesh['leaf'=8,'front'=16] {'leaf'}, use_global_device_ids=true, to_apply=%region_10.13 | all-reduce | flops 16384 | bytes 65536 | tf_op jit(solution)/shard_map/psum | solution.py:11
  702.2 54.4 %all-reduce.27.cloned.1.call-done = bf16[1024,128]{1,0:T(8,128)(2,1)} async-done(((bf16[1024,128]{1,0:T(8,128)(2,1)}), bf16[1024,128]{1,0:T(8,128)(2,1)}) %all-reduce.27.cloned.1.call-update) | async-done | bytes 262160 | tf_op jit(solution)/shard_map/psum | solution.py:11
  768.2 84.8 %all-reduce.29.cloned.1.call-done = bf16[2048,128]{0,1:T(8,128)(2,1)} async-done(((bf16[2048,128]{0,1:T(8,128)(2,1)}), bf16[2048,128]{0,1:T(8,128)(2,1)}) %all-reduce.29.cloned.1.call-update) | async-done | bytes 524304 | tf_op jit(solution)/shard_map/psum | solution.py:11
  853.8 24.0 %psum.178 = bf16[128,128]{0,1:T(8,128)(2,1)S(1)} all-reduce(bf16[128,128]{0,1:T(8,128)(2,1)S(1)} %slice_select_fusion.4), channel_id=1, replica_groups=mesh['leaf'=8,'front'=16] {'leaf'}, use_global_device_ids=true, to_apply=%region_13.16 | all-reduce | flops 16384 | bytes 65536 | tf_op jit(solution)/shard_map/psum | solution.py:11
  910.3 54.3 %all-reduce.31.cloned.1.call-done = bf16[1024,128]{1,0:T(8,128)(2,1)} async-done(((bf16[1024,128]{1,0:T(8,128)(2,1)}), bf16[1024,128]{1,0:T(8,128)(2,1)}) %all-reduce.31.cloned.1.call-update) | async-done | bytes 262160 | tf_op jit(solution)/shard_map/psum | solution.py:11
  976.3 84.9 %all-reduce.33.cloned.1.call-done = bf16[2048,128]{0,1:T(8,128)(2,1)} async-done(((bf16[2048,128]{0,1:T(8,128)(2,1)}), bf16[2048,128]{0,1:T(8,128)(2,1)}) %all-reduce.33.cloned.1.call-update) | async-done | bytes 524304 | tf_op jit(solution)/shard_map/psum | solution.py:11
  1061.9 24.1 %psum.181 = bf16[128,128]{0,1:T(8,128)(2,1)S(1)} all-reduce(bf16[128,128]{0,1:T(8,128)(2,1)S(1)} %slice_select_fusion.3), channel_id=1, replica_groups=mesh['leaf'=8,'front'=16] {'leaf'}, use_global_device_ids=true, to_apply=%region_16.19 | all-reduce | flops 16384 | bytes 65536 | tf_op jit(solution)/shard_map/psum | solution.py:11
  1118.6 54.4 %all-reduce.35.cloned.1.call-done = bf16[1024,128]{1,0:T(8,128)(2,1)} async-done(((bf16[1024,128]{1,0:T(8,128)(2,1)}), bf16[1024,128]{1,0:T(8,128)(2,1)}) %all-reduce.35.cloned.1.call-update) | async-done | bytes 262160 | tf_op jit(solution)/shard_map/psum | solution.py:11
  1184.6 84.8 %all-reduce.37.cloned.1.call-done = bf16[2048,128]{0,1:T(8,128)(2,1)} async-done(((bf16[2048,128]{0,1:T(8,128)(2,1)}), bf16[2048,128]{0,1:T(8,128)(2,1)}) %all-reduce.37.cloned.1.call-update) | async-done | bytes 524304 | tf_op jit(solution)/shard_map/psum | solution.py:11
  1326.6 54.4 %all-reduce.39.cloned.1.call-done = bf16[1024,128]{1,0:T(8,128)(2,1)} async-done(((bf16[1024,128]{1,0:T(8,128)(2,1)}), bf16[1024,128]{1,0:T(8,128)(2,1)}) %all-reduce.39.cloned.1.call-update) | async-done | bytes 262160 | tf_op jit(solution)/shard_map/psum | solution.py:11
  1392.7 84.8 %all-reduce.41.cloned.1.call-done = bf16[2048,128]{0,1:T(8,128)(2,1)} async-done(((bf16[2048,128]{0,1:T(8,128)(2,1)}), bf16[2048,128]{0,1:T(8,128)(2,1)}) %all-reduce.41.cloned.1.call-update) | async-done | bytes 524304 | tf_op jit(solution)/shard_map/psum | solution.py:11
  1478.3 24.0 %psum.187 = bf16[128,128]{0,1:T(8,128)(2,1)S(1)} all-reduce(bf16[128,128]{0,1:T(8,128)(2,1)S(1)} %slice_select_fusion.1), channel_id=1, replica_groups=mesh['leaf'=8,'front'=16] {'leaf'}, use_global_device_ids=true, to_apply=%region_22.25 | all-reduce | flops 16384 | bytes 65536 | tf_op jit(solution)/shard_map/psum | solution.py:11
  1534.7 54.3 %all-reduce.43.cloned.1.call-done = bf16[1024,128]{1,0:T(8,128)(2,1)} async-done(((bf16[1024,128]{1,0:T(8,128)(2,1)}), bf16[1024,128]{1,0:T(8,128)(2,1)}) %all-reduce.43.cloned.1.call-update) | async-done | bytes 262160 | tf_op jit(solution)/shard_map/psum | solution.py:11
  1600.7 84.8 %all-reduce.45.cloned.1.call-done = bf16[2048,128]{0,1:T(8,128)(2,1)} async-done(((bf16[2048,128]{0,1:T(8,128)(2,1)}), bf16[2048,128]{0,1:T(8,128)(2,1)}) %all-reduce.45.cloned.1.call-update) | async-done | bytes 524304 | tf_op jit(solution)/shard_map/psum | solution.py:11
  1686.3 24.1 %psum.190 = bf16[128,128]{0,1:T(8,128)(2,1)S(1)} all-reduce(bf16[128,128]{0,1:T(8,128)(2,1)S(1)} %slice_select_fusion), channel_id=1, replica_groups=mesh['leaf'=8,'front'=16] {'leaf'}, use_global_device_ids=true, to_apply=%region_25.28 | all-reduce | flops 16384 | bytes 65536 | tf_op jit(solution)/shard_map/psum | solution.py:11
  1742.9 54.5 %all-reduce.47.cloned.1.call-done = bf16[1024,128]{1,0:T(8,128)(2,1)} async-done(((bf16[1024,128]{1,0:T(8,128)(2,1)}), bf16[1024,128]{1,0:T(8,128)(2,1)}) %all-reduce.47.cloned.1.call-update) | async-done | bytes 262160 | tf_op jit(solution)/shard_map/psum | solution.py:11
  (234 shorter events, 490.5 us)
Async XLA Ops:
  6.5 50.5 %all-gather.5.cloned.1.call-start = ((), (), s32[]{:S(2)}) async-start(), calls=%async_computation.16 | async-start | bytes 2228224 | tf_op jit(solution)/shard_map/all_gather | solution.py:31
  7.3 84.5 %all-gather.7.cloned.1.call-start = ((), (), s32[]{:S(2)}) async-start(), calls=%async_computation.17 | async-start | bytes 4718592 | tf_op jit(solution)/shard_map/all_gather | solution.py:47
  60.3 170.3 %all-reduce.17.cloned.1.call-start = ((), (), s32[]{:S(2)}) async-start(), calls=%async_computation | async-start | bytes 1048576 | tf_op jit(solution)/shard_map/psum | solution.py:11
  70.3 9.2 copy-start.7
  144.7 195.6 %all-reduce.19.cloned.1.call-start = ((), (), s32[]{:S(2)}) async-start(), calls=%async_computation.1 | async-start | bytes 524288 | tf_op jit(solution)/shard_map/psum | solution.py:11
  282.8 153.9 %all-reduce.21.cloned.1.call-start = ((), (), s32[]{:S(2)}) async-start(), calls=%async_computation.2 | async-start | bytes 1048576 | tf_op jit(solution)/shard_map/psum | solution.py:11
  346.6 3.4 copy-start.2
  351.8 196.7 %all-reduce.23.cloned.1.call-start = ((), (), s32[]{:S(2)}) async-start(), calls=%async_computation.3 | async-start | bytes 524288 | tf_op jit(solution)/shard_map/psum | solution.py:11
  491.1 153.9 %all-reduce.25.cloned.1.call-start = ((), (), s32[]{:S(2)}) async-start(), calls=%async_computation.4 | async-start | bytes 1048576 | tf_op jit(solution)/shard_map/psum | solution.py:11
  554.9 3.4 copy-start.3
  560.0 196.6 %all-reduce.27.cloned.1.call-start = ((), (), s32[]{:S(2)}) async-start(), calls=%async_computation.5 | async-start | bytes 524288 | tf_op jit(solution)/shard_map/psum | solution.py:11
  699.1 154.0 %all-reduce.29.cloned.1.call-start = ((), (), s32[]{:S(2)}) async-start(), calls=%async_computation.6 | async-start | bytes 1048576 | tf_op jit(solution)/shard_map/psum | solution.py:11
  762.9 3.4 copy-start.4
  768.1 196.6 %all-reduce.31.cloned.1.call-start = ((), (), s32[]{:S(2)}) async-start(), calls=%async_computation.7 | async-start | bytes 524288 | tf_op jit(solution)/shard_map/psum | solution.py:11
  907.2 153.9 %all-reduce.33.cloned.1.call-start = ((), (), s32[]{:S(2)}) async-start(), calls=%async_computation.8 | async-start | bytes 1048576 | tf_op jit(solution)/shard_map/psum | solution.py:11
  971.0 3.4 copy-start.5
  976.1 196.9 %all-reduce.35.cloned.1.call-start = ((), (), s32[]{:S(2)}) async-start(), calls=%async_computation.9 | async-start | bytes 524288 | tf_op jit(solution)/shard_map/psum | solution.py:11
  1115.5 154.0 %all-reduce.37.cloned.1.call-start = ((), (), s32[]{:S(2)}) async-start(), calls=%async_computation.10 | async-start | bytes 1048576 | tf_op jit(solution)/shard_map/psum | solution.py:11
  1184.4 196.6 %all-reduce.39.cloned.1.call-start = ((), (), s32[]{:S(2)}) async-start(), calls=%async_computation.11 | async-start | bytes 524288 | tf_op jit(solution)/shard_map/psum | solution.py:11
  1323.5 153.9 %all-reduce.41.cloned.1.call-start = ((), (), s32[]{:S(2)}) async-start(), calls=%async_computation.12 | async-start | bytes 1048576 | tf_op jit(solution)/shard_map/psum | solution.py:11
  1387.4 3.4 copy-start
  1392.5 196.6 %all-reduce.43.cloned.1.call-start = ((), (), s32[]{:S(2)}) async-start(), calls=%async_computation.13 | async-start | bytes 524288 | tf_op jit(solution)/shard_map/psum | solution.py:11
  1531.7 153.9 %all-reduce.45.cloned.1.call-start = ((), (), s32[]{:S(2)}) async-start(), calls=%async_computation.14 | async-start | bytes 1048576 | tf_op jit(solution)/shard_map/psum | solution.py:11
  1600.5 196.9 %all-reduce.47.cloned.1.call-start = ((), (), s32[]{:S(2)}) async-start(), calls=%async_computation.15 | async-start | bytes 524288 | tf_op jit(solution)/shard_map/psum | solution.py:11
  (2 other events, 6.8 us)
Sparse Core Ops, SparseCore 0:
  9.5 47.4 all-gather.4
  60.4 31.3 all-gather.6
  144.8 85.7 all-reduce.16
  282.9 57.3 all-reduce.18
  351.9 84.8 all-reduce.20
  491.2 57.2 all-reduce.22
  560.1 84.8 all-reduce.24
  699.2 57.3 all-reduce.26
  768.2 84.8 all-reduce.28
  907.3 57.2 all-reduce.30
  976.2 84.8 all-reduce.32
  1115.6 57.3 all-reduce.34
  1184.6 84.8 all-reduce.36
  1323.7 57.3 all-reduce.38
  1392.6 84.8 all-reduce.40
  1531.8 57.2 all-reduce.42
  1600.6 84.8 all-reduce.44
  1740.0 57.3 all-reduce.46
where the time goes:
time: 1850 us; the launch traced here: 1840 us
  waiting for transfers between devices  1180 us (64%)
  other arithmetic  258 us (14%)
  blocking collectives  192 us (10%)
  local copies, waits for them, and re-layouts  114 us (6%)
  matrix products  81.6 us (4%)
    psum x16, waiting for transfers between devices, broadcast(): return lax.psum(jnp.where(mine, x, jnp.zeros_like(x)), axis)  1120 us
    psum x8, blocking collectives, broadcast(): return lax.psum(jnp.where(mine, x, jnp.zeros_like(x)), axis)  192 us
    another operation x24, other arithmetic, on_device(): factor = jnp.linalg.cholesky(pivot)  99.8 us
    another operation x16, other arithmetic, on_device(): lax.linalg.triangular_solve(factor, panel, left_side=False, lower=True, t...  84.1 us
    dot_general x8, matrix products, on_device(): lax.dot_general(solved, matching.reshape(col_blocks * block_size, block_s...  50.9 us
    all_gather x1, waiting for transfers between devices, on_device(): lax.all_gather(child_panels[0], 'front', axis=0, tiled=True)  49.7 us
    unnamed x26, local copies, waits for them, and re-layouts  47.1 us
  transfers between devices with their start and end apart: 18, of which 18 were waited for; matrix products, arithmetic and copies ran while one was open for 2% of the time, Pallas kernels for 0%

commit v1 on v0

--- a/solution.py
+++ b/solution.py
@@ -8,7 +8,7 @@
 
 def broadcast(x, axis, root):
     mine = lax.axis_index(axis) == root
-    return lax.psum(jnp.where(mine, x, jnp.zeros_like(x)), axis)
+    return jnp.sum(lax.all_gather(jnp.where(mine, x, jnp.zeros_like(x)), axis_name=axis), 0)
 
 
 def for_sending(x):

time: 1850 us -> 1520 us (0.82)
  waiting for transfers between devices: 1180 us -> 802 us
  blocking collectives: 192 us -> 99.9 us
  other arithmetic: 258 us -> 328 us
  local copies, waits for them, and re-layouts: 114 us -> 184 us
    psum x16 -> x0, waiting for transfers between devices: 1120 us -> none  [broadcast(): return lax.psum(jnp.where(mine, x, jnp.zeros_like(x)), axis)]
    all_gather x0 -> x16, waiting for transfers between devices: none -> 739 us  [broadcast(): lax.all_gather(jnp.where(mine, x, jnp.zeros_like(x)), axis_name=axis)]
    psum x8 -> x0, blocking collectives: 192 us -> none  [broadcast(): return lax.psum(jnp.where(mine, x, jnp.zeros_like(x)), axis)]
    all_gather x0 -> x8, blocking collectives: none -> 99.9 us  [broadcast(): lax.all_gather(jnp.where(mine, x, jnp.zeros_like(x)), axis_name=axis)]
    unnamed x26 -> x34, local copies, waits for them, and re-layouts: 47.1 us -> 141 us
    reduce_sum x0 -> x24, other arithmetic: none -> 77.5 us  [broadcast(): jnp.sum(lax.all_gather(jnp.where(mine, x, jnp.zeros_like(x)), axis_name=a...]
    transpose x1 -> x0, local copies, waits for them, and re-layouts: 25.1 us -> none  [on_device(): jnp.einsum('cqr,cqxy,cs->rxsy', row_onehot, received.astype(jnp.float32),...]
  transfers between devices with their start and end apart: 18 -> 18, of which waited for: 18 -> 18; matrix products, arithmetic and copies ran while one was open for 2% -> 3% of each run, Pallas kernels for 0% -> 0%
where the time goes in v1:
time: 1520 us; the launch traced here: 1510 us
  waiting for transfers between devices  802 us (53%)
  other arithmetic  328 us (22%)
  local copies, waits for them, and re-layouts  184 us (12%)
  blocking collectives  99.9 us (7%)
  matrix products  73.3 us (5%)
    all_gather x16, waiting for transfers between devices, broadcast(): lax.all_gather(jnp.where(mine, x, jnp.zeros_like(x)), axis_name=axis)  739 us
    unnamed x34, local copies, waits for them, and re-layouts  141 us
    all_gather x8, blocking collectives, broadcast(): lax.all_gather(jnp.where(mine, x, jnp.zeros_like(x)), axis_name=axis)  99.9 us
    another operation x24, other arithmetic, on_device(): factor = jnp.linalg.cholesky(pivot)  99.7 us
    another operation x16, other arithmetic, on_device(): lax.linalg.triangular_solve(factor, panel, left_side=False, lower=True, t...  84.1 us
    reduce_sum x24, other arithmetic, broadcast(): jnp.sum(lax.all_gather(jnp.where(mine, x, jnp.zeros_like(x)), axis_name=a...  77.5 us
    dot_general x8, matrix products, on_device(): lax.dot_general(solved, matching.reshape(col_blocks * block_size, block_s...  50.9 us
    all_gather x1, waiting for transfers between devices, on_device(): lax.all_gather(child_panels[0], 'front', axis=0, tiled=True)  49.7 us
  transfers between devices with their start and end apart: 18, of which 18 were waited for; matrix products, arithmetic and copies ran while one was open for 3% of the time, Pallas kernels for 0%

profile of v1, /device:TPU:0, one launch (start us, length us, event | category | flops | bytes accessed | tf_op | source)
XLA Modules:
  0.0 1505.4 jit_solution(13356152838877306854)
XLA Ops:
  7.3 49.7 %all-gather.45.cloned.1.call-done = bf16[1,2048,512]{2,1,0:T(8,128)(2,1)} async-done(((bf16[1,128,512]{2,1,0:T(8,128)(2,1)}), bf16[1,2048,512]{2,1,0:T(8,128)(2,1)}) %all-gather.45.cloned.1.call-update) | async-done | bytes 2097168 | tf_op jit(solution)/shard_map/all_gather | solution.py:31
  103.6 14.1 copy.98
  117.7 13.9 bitcast_add_fusion
  133.9 70.9 %all-gather.49.cloned.1.call-done = bf16[32768,128]{0,1:T(8,128)(2,1)} async-done(((bf16[2048,128]{0,1:T(8,128)(2,1)}), bf16[32768,128]{0,1:T(8,128)(2,1)}) %all-gather.49.cloned.1.call-update) | async-done | bytes 8388624 | tf_op jit(solution)/shard_map/all_gather | solution.py:11
  204.8 12.9 copy.110
  264.0 23.3 %all-gather.51.cloned.1.call-done = bf16[64,1,128,128]{3,2,1,0:T(8,128)(2,1)} async-done(((bf16[8,1,128,128]{3,2,1,0:T(8,128)(2,1)}), bf16[64,1,128,128]{3,2,1,0:T(8,128)(2,1)}) %all-gather.51.cloned.1.call-update) | async-done | bytes 2097168 | tf_op jit(solution)/shard_map/all_gather | solution.py:11
  301.0 71.1 %all-gather.53.cloned.1.call-done = bf16[32768,128]{0,1:T(8,128)(2,1)} async-done(((bf16[2048,128]{0,1:T(8,128)(2,1)}), bf16[32768,128]{0,1:T(8,128)(2,1)}) %all-gather.53.cloned.1.call-update) | async-done | bytes 8388624 | tf_op jit(solution)/shard_map/all_gather | solution.py:11
  372.2 12.9 copy.112
  433.9 21.0 %all-gather.55.cloned.1.call-done = bf16[64,1,128,128]{3,2,1,0:T(8,128)(2,1)} async-done(((bf16[8,1,128,128]{3,2,1,0:T(8,128)(2,1)}), bf16[64,1,128,128]{3,2,1,0:T(8,128)(2,1)}) %all-gather.55.cloned.1.call-update) | async-done | bytes 2097168 | tf_op jit(solution)/shard_map/all_gather | solution.py:11
  468.6 71.1 %all-gather.57.cloned.1.call-done = bf16[32768,128]{0,1:T(8,128)(2,1)} async-done(((bf16[2048,128]{0,1:T(8,128)(2,1)}), bf16[32768,128]{0,1:T(8,128)(2,1)}) %all-gather.57.cloned.1.call-update) | async-done | bytes 8388624 | tf_op jit(solution)/shard_map/all_gather | solution.py:11
  539.7 12.9 copy.114
  601.3 21.1 %all-gather.59.cloned.1.call-done = bf16[64,1,128,128]{3,2,1,0:T(8,128)(2,1)} async-done(((bf16[8,1,128,128]{3,2,1,0:T(8,128)(2,1)}), bf16[64,1,128,128]{3,2,1,0:T(8,128)(2,1)}) %all-gather.59.cloned.1.call-update) | async-done | bytes 2097168 | tf_op jit(solution)/shard_map/all_gather | solution.py:11
  636.2 70.9 %all-gather.61.cloned.1.call-done = bf16[32768,128]{0,1:T(8,128)(2,1)} async-done(((bf16[2048,128]{0,1:T(8,128)(2,1)}), bf16[32768,128]{0,1:T(8,128)(2,1)}) %all-gather.61.cloned.1.call-update) | async-done | bytes 8388624 | tf_op jit(solution)/shard_map/all_gather | solution.py:11
  707.1 12.9 copy.116
  768.7 21.0 %all-gather.63.cloned.1.call-done = bf16[64,1,128,128]{3,2,1,0:T(8,128)(2,1)} async-done(((bf16[8,1,128,128]{3,2,1,0:T(8,128)(2,1)}), bf16[64,1,128,128]{3,2,1,0:T(8,128)(2,1)}) %all-gather.63.cloned.1.call-update) | async-done | bytes 2097168 | tf_op jit(solution)/shard_map/all_gather | solution.py:11
  803.4 71.1 %all-gather.65.cloned.1.call-done = bf16[32768,128]{0,1:T(8,128)(2,1)} async-done(((bf16[2048,128]{0,1:T(8,128)(2,1)}), bf16[32768,128]{0,1:T(8,128)(2,1)}) %all-gather.65.cloned.1.call-update) | async-done | bytes 8388624 | tf_op jit(solution)/shard_map/all_gather | solution.py:11
  936.3 21.0 %all-gather.67.cloned.1.call-done = bf16[64,1,128,128]{3,2,1,0:T(8,128)(2,1)} async-done(((bf16[8,1,128,128]{3,2,1,0:T(8,128)(2,1)}), bf16[64,1,128,128]{3,2,1,0:T(8,128)(2,1)}) %all-gather.67.cloned.1.call-update) | async-done | bytes 2097168 | tf_op jit(solution)/shard_map/all_gather | solution.py:11
  970.9 71.1 %all-gather.69.cloned.1.call-done = bf16[32768,128]{0,1:T(8,128)(2,1)} async-done(((bf16[2048,128]{0,1:T(8,128)(2,1)}), bf16[32768,128]{0,1:T(8,128)(2,1)}) %all-gather.69.cloned.1.call-update) | async-done | bytes 8388624 | tf_op jit(solution)/shard_map/all_gather | solution.py:11
  1103.7 21.0 %all-gather.71.cloned.1.call-done = bf16[64,1,128,128]{3,2,1,0:T(8,128)(2,1)} async-done(((bf16[8,1,128,128]{3,2,1,0:T(8,128)(2,1)}), bf16[64,1,128,128]{3,2,1,0:T(8,128)(2,1)}) %all-gather.71.cloned.1.call-update) | async-done | bytes 2097168 | tf_op jit(solution)/shard_map/all_gather | solution.py:11
  1138.6 70.9 %all-gather.73.cloned.1.call-done = bf16[32768,128]{0,1:T(8,128)(2,1)} async-done(((bf16[2048,128]{0,1:T(8,128)(2,1)}), bf16[32768,128]{0,1:T(8,128)(2,1)}) %all-gather.73.cloned.1.call-update) | async-done | bytes 8388624 | tf_op jit(solution)/shard_map/all_gather | solution.py:11
  1271.0 21.1 %all-gather.75.cloned.1.call-done = bf16[64,1,128,128]{3,2,1,0:T(8,128)(2,1)} async-done(((bf16[8,1,128,128]{3,2,1,0:T(8,128)(2,1)}), bf16[64,1,128,128]{3,2,1,0:T(8,128)(2,1)}) %all-gather.75.cloned.1.call-update) | async-done | bytes 2097168 | tf_op jit(solution)/shard_map/all_gather | solution.py:11
  1305.7 71.1 %all-gather.77.cloned.1.call-done = bf16[32768,128]{0,1:T(8,128)(2,1)} async-done(((bf16[2048,128]{0,1:T(8,128)(2,1)}), bf16[32768,128]{0,1:T(8,128)(2,1)}) %all-gather.77.cloned.1.call-update) | async-done | bytes 8388624 | tf_op jit(solution)/shard_map/all_gather | solution.py:11
  1438.5 21.0 %all-gather.79.cloned.1.call-done = bf16[64,1,128,128]{3,2,1,0:T(8,128)(2,1)} async-done(((bf16[8,1,128,128]{3,2,1,0:T(8,128)(2,1)}), bf16[64,1,128,128]{3,2,1,0:T(8,128)(2,1)}) %all-gather.79.cloned.1.call-update) | async-done | bytes 2097168 | tf_op jit(solution)/shard_map/all_gather | solution.py:11
  1474.3 13.3 copy.86
  (257 shorter events, 608.8 us)
Async XLA Ops:
  6.5 50.5 %all-gather.45.cloned.1.call-start = ((), (), s32[]{:S(2)}) async-start(), calls=%async_computation | async-start | bytes 2228224 | tf_op jit(solution)/shard_map/all_gather | solution.py:31
  7.3 84.5 %all-gather.47.cloned.1.call-start = ((), (), s32[]{:S(2)}) async-start(), calls=%async_computation.1 | async-start | bytes 4718592 | tf_op jit(solution)/shard_map/all_gather | solution.py:47
  60.3 144.4 %all-gather.49.cloned.1.call-start = ((), (), s32[]{:S(2)}) async-start(), calls=%async_computation.2 | async-start | bytes 8912896 | tf_op jit(solution)/shard_map/all_gather | solution.py:11
  69.2 9.3 copy-start.7
  133.7 153.7 %all-gather.51.cloned.1.call-start = ((), (), s32[]{:S(2)}) async-start(), calls=%async_computation.3 | async-start | bytes 2359296 | tf_op jit(solution)/shard_map/all_gather | solution.py:11
  263.3 108.9 %all-gather.53.cloned.1.call-start = ((), (), s32[]{:S(2)}) async-start(), calls=%async_computation.4 | async-start | bytes 8912896 | tf_op jit(solution)/shard_map/all_gather | solution.py:11
  295.7 3.4 copy-start.1
  300.7 154.3 %all-gather.55.cloned.1.call-start = ((), (), s32[]{:S(2)}) async-start(), calls=%async_computation.5 | async-start | bytes 2359296 | tf_op jit(solution)/shard_map/all_gather | solution.py:11
  430.9 108.8 %all-gather.57.cloned.1.call-start = ((), (), s32[]{:S(2)}) async-start(), calls=%async_computation.6 | async-start | bytes 8912896 | tf_op jit(solution)/shard_map/all_gather | solution.py:11
  463.3 3.4 copy-start.2
  468.3 154.1 %all-gather.59.cloned.1.call-start = ((), (), s32[]{:S(2)}) async-start(), calls=%async_computation.7 | async-start | bytes 2359296 | tf_op jit(solution)/shard_map/all_gather | solution.py:11
  598.3 108.9 %all-gather.61.cloned.1.call-start = ((), (), s32[]{:S(2)}) async-start(), calls=%async_computation.8 | async-start | bytes 8912896 | tf_op jit(solution)/shard_map/all_gather | solution.py:11
  635.7 154.1 %all-gather.63.cloned.1.call-start = ((), (), s32[]{:S(2)}) async-start(), calls=%async_computation.9 | async-start | bytes 2359296 | tf_op jit(solution)/shard_map/all_gather | solution.py:11
  765.6 108.8 %all-gather.65.cloned.1.call-start = ((), (), s32[]{:S(2)}) async-start(), calls=%async_computation.10 | async-start | bytes 8912896 | tf_op jit(solution)/shard_map/all_gather | solution.py:11
  798.0 3.4 copy-start.4
  803.0 154.3 %all-gather.67.cloned.1.call-start = ((), (), s32[]{:S(2)}) async-start(), calls=%async_computation.11 | async-start | bytes 2359296 | tf_op jit(solution)/shard_map/all_gather | solution.py:11
  933.2 108.9 %all-gather.69.cloned.1.call-start = ((), (), s32[]{:S(2)}) async-start(), calls=%async_computation.12 | async-start | bytes 8912896 | tf_op jit(solution)/shard_map/all_gather | solution.py:11
  965.6 3.4 copy-start.5
  970.6 154.1 %all-gather.71.cloned.1.call-start = ((), (), s32[]{:S(2)}) async-start(), calls=%async_computation.13 | async-start | bytes 2359296 | tf_op jit(solution)/shard_map/all_gather | solution.py:11
  1100.6 108.8 %all-gather.73.cloned.1.call-start = ((), (), s32[]{:S(2)}) async-start(), calls=%async_computation.14 | async-start | bytes 8912896 | tf_op jit(solution)/shard_map/all_gather | solution.py:11
  1133.0 3.4 copy-start.6
  1138.0 154.1 %all-gather.75.cloned.1.call-start = ((), (), s32[]{:S(2)}) async-start(), calls=%async_computation.15 | async-start | bytes 2359296 | tf_op jit(solution)/shard_map/all_gather | solution.py:11
  1268.0 108.9 %all-gather.77.cloned.1.call-start = ((), (), s32[]{:S(2)}) async-start(), calls=%async_computation.16 | async-start | bytes 8912896 | tf_op jit(solution)/shard_map/all_gather | solution.py:11
  1305.4 154.1 %all-gather.79.cloned.1.call-start = ((), (), s32[]{:S(2)}) async-start(), calls=%async_computation.17 | async-start | bytes 2359296 | tf_op jit(solution)/shard_map/all_gather | solution.py:11
  (2 other events, 6.8 us)
Sparse Core Ops, SparseCore 0:
  9.5 47.4 all-gather.44
  60.4 31.3 all-gather.46
  133.9 70.8 all-gather.48
  263.4 23.9 all-gather.50
  300.8 71.2 all-gather.52
  431.0 23.9 all-gather.54
  468.4 71.2 all-gather.56
  598.4 23.9 all-gather.58
  635.8 71.2 all-gather.60
  765.8 23.9 all-gather.62
  803.1 71.2 all-gather.64
  933.3 23.9 all-gather.66
  970.7 71.2 all-gather.68
  1100.7 23.9 all-gather.70
  1138.1 71.2 all-gather.72
  1268.1 23.9 all-gather.74
  1305.5 71.2 all-gather.76
  1435.5 23.9 all-gather.78
